TPU v7x, 256 devices: a whole 4x4x8 slice. The times are simulated.
256 devices in a mesh: dp: 8 (over z_lo, core), seq: 16 (over x, y), mp: 2 (over z_hi).
Axes of the slice: x: 4, y: 4, z: 8 (z_hi: 2, z_lo: 4; z = z_hi * 4 + z_lo), core: 2. Of those that a mesh axis runs over, the one named last changes fastest.
Arguments:
- features: bfloat16 [8, 8192, 1408], P('dp', ('seq', 'mp')), may hold values from -6 to 6
- conv_weight: bfloat16 [5, 1408, 1536], P(None, ('seq', 'mp')), may hold values from -0.0625 to 0.0625
- norm_gain: float32 [1536], replicated, may hold values from 0.25 to 1.75
- query_weight: bfloat16 [1536, 1024], replicated, may hold values from -0.15625 to 0.15625
- keyval_weight: bfloat16 [1536, 320], replicated, may hold values from -0.15625 to 0.15625
- head_scale: float32 [8], replicated, may hold values from 0.5 to 24
- output_weight: bfloat16 [1536, 1536], replicated, may hold values from -0.15625 to 0.15625
- pair_weight: bfloat16 [1536, 256], replicated, may hold values from -0.625 to 0.625
- pair_input: bfloat16 [8, 256, 256, 128], P('dp', ('seq', 'mp')), may hold values from -6 to 6
- flip_weight: bfloat16 [128, 128], replicated, may hold values from -0.5 to 0.5
- pair_cotangent: bfloat16 [8, 256, 256, 128], P('dp', ('seq', 'mp')), may hold values from -0.0234375 to 0.0234375
Outputs:
- block_out: bfloat16 [8, 4096, 1536], P('dp', ('seq', 'mp'))
- pair_out: bfloat16 [8, 256, 256, 128], P('dp', ('seq', 'mp'))
- grad_flip: float32 [128, 128], replicated
All inputs are finite; a program needn't handle non-finite values.
Results may differ from a plain program's by a relative error of at most 0.011.
Values may be sent and summed in bfloat16 or wider, within the bound.
A program may use at most 192 MiB of HBM per device.

v0:
```python
import math
import jax
import jax.numpy as jnp
from jax import lax
from jax.sharding import PartitionSpec as P

PAIR_POOL = 16
norm_eps = 1e-06
logit_cap = 50.0


def padded_2(shard, sides, width):
    for axis, dim in sides:
        devices, length = (lax.axis_size(axis), shard.shape[dim])
        up = [(i, (i + 1) % devices) for i in range(devices - 1)]
        down = [(j, i) for i, j in up]
        last = lax.slice_in_dim(shard, length - width, length, axis=dim)
        initial = lax.slice_in_dim(shard, 0, width, axis=dim)
        before = lax.ppermute(last, axis, up)
        after = lax.ppermute(initial, axis, down)
        shard = jnp.concatenate([before, shard, after], axis=dim)
    return shard


def root_norm(values_in):
    return values_in * lax.rsqrt(jnp.mean(values_in * values_in, axis=-1, keepdims=True) + norm_eps)


def prepare(raw):
    return jax.nn.gelu(root_norm(raw.astype(jnp.float32)), approximate=False).astype(jnp.bfloat16)


def tap_sum(source, out_rows, tap_count, running, filter_rows):
    for lag_index in range(tap_count):
        running = running + jnp.dot(
            source[lag_index : lag_index + out_rows],
            filter_rows[lag_index],
            preferred_element_type=jnp.float32,
        )
    return running


def per_device(
    features,
    conv_weight,
    norm_gain,
    query_weight,
    keyval_weight,
    head_scale,
    output_weight,
    pair_weight,
    pair_input,
    flip_weight,
    pair_cotangent,
):
    fine_rows = features.shape[1]
    coarse_rows = fine_rows // 2
    in_channels = features.shape[2]
    model_dim = output_weight.shape[1]
    head_count = head_scale.shape[0]
    key_dim = query_weight.shape[1] // head_count
    pair_dim = flip_weight.shape[0]
    tap_count = conv_weight.shape[0]
    margin = tap_count // 2
    padded = padded_2(features, ((("seq", "mp"), 1),), margin)
    prepared = prepare(padded[0])
    starting = jnp.zeros((fine_rows, model_dim), jnp.float32)
    conv_sum = tap_sum(
        prepared,
        fine_rows,
        tap_count,
        starting,
        lax.all_gather(conv_weight, ("seq", "mp"), axis=1, tiled=True),
    )
    skipped = jnp.pad(features[0].astype(jnp.float32), ((0, 0), (0, model_dim - in_channels)))
    encoded = jnp.max((conv_sum + skipped).reshape(coarse_rows, 2, model_dim), axis=1).astype(
        jnp.bfloat16
    )
    widened = encoded.astype(jnp.float32)
    normed = (root_norm(widened) * norm_gain).astype(jnp.bfloat16)
    scale_row = jnp.repeat(head_scale, key_dim) / math.sqrt(key_dim)
    queries = (
        jnp.dot(normed, query_weight, preferred_element_type=jnp.float32) * scale_row
    ).astype(jnp.bfloat16)
    keyvals = jnp.dot(normed, keyval_weight, preferred_element_type=jnp.float32).astype(
        jnp.bfloat16
    )
    pooled = jnp.mean(
        widened.reshape(coarse_rows // PAIR_POOL, PAIR_POOL, model_dim), axis=1
    ).astype(jnp.bfloat16)
    pair_feats = jnp.dot(pooled, pair_weight, preferred_element_type=jnp.float32).astype(
        jnp.bfloat16
    )
    pair_q = pair_feats[:, :pair_dim]
    pair_k = pair_feats[:, pair_dim:]
    keys_all, pairk_all = (
        lax.all_gather(keyvals[None], ("seq", "mp"), axis=1, tiled=True),
        lax.all_gather(pair_k[None], ("seq", "mp"), axis=1, tiled=True),
    )
    summed = (
        pair_input[0].astype(jnp.float32)
        + pair_q[:, None, :].astype(jnp.float32) * pairk_all[0][None, :, :].astype(jnp.float32)
    ).astype(jnp.bfloat16)
    flipped = lax.all_to_all(summed[None], ("seq", "mp"), split_axis=2, concat_axis=1, tiled=True)[
        0
    ]
    turned = jnp.einsum("bac,cd->abd", flipped, flip_weight, preferred_element_type=jnp.float32)
    pair_out = (summed.astype(jnp.float32) + turned).astype(jnp.bfloat16)
    grad_term = jnp.einsum(
        "bac,abd->cd", flipped, pair_cotangent[0], preferred_element_type=jnp.float32
    )
    grad_flip = lax.psum(grad_term, ("dp", "seq", "mp"))
    key_rows = keys_all[0][:, :key_dim]
    value_rows = keys_all[0][:, key_dim:]
    query_rows = queries.reshape(coarse_rows * head_count, key_dim)
    scores = jnp.dot(query_rows, key_rows.T, preferred_element_type=jnp.float32)
    weights = jnp.exp(logit_cap * jnp.tanh(scores / logit_cap))
    totals = jnp.sum(weights, axis=-1, keepdims=True)
    mixed = (
        jnp.dot(weights.astype(jnp.bfloat16), value_rows, preferred_element_type=jnp.float32)
        / totals
    )
    heads_out = mixed.astype(jnp.bfloat16).reshape(coarse_rows, head_count * value_rows.shape[1])
    block_out = (
        widened + jnp.dot(heads_out, output_weight, preferred_element_type=jnp.float32)
    ).astype(jnp.bfloat16)
    return (block_out[None], pair_out[None], grad_flip)


def solution(mesh):
    placed = (
        P("dp", ("seq", "mp"), None),
        P(None, ("seq", "mp"), None),
        P(),
        P(),
        P(),
        P(),
        P(),
        P(),
        P("dp", ("seq", "mp"), None, None),
        P(),
        P("dp", ("seq", "mp"), None, None),
    )
    return jax.shard_map(
        per_device,
        mesh=mesh,
        in_specs=placed,
        out_specs=(P("dp", ("seq", "mp"), None), P("dp", ("seq", "mp"), None, None), P()),
        check_vma=False,
    )
```

profile of v0, /device:TPU:1, one launch (start us, length us, event | category | flops | bytes accessed | tf_op | source)
XLA Modules:
  0.0 959.2 jit_solution(9439417309653292819)
XLA Ops:
  7.2 0.0 copy-start
  7.2 0.0 all-gather.5.cloned.1.call-start
  7.2 2.7 copy.24
  9.9 0.0 all-gather.5.cloned.1.call-update
  9.9 0.0 all-gather.7.cloned.1.call-start
  10.0 0.8 fusion.84
  10.7 1.3 collective-permute-start.1
  12.0 10.3 %collective-permute-start = (bf16[1,2,1408]{2,1,0:T(2,128)(2,1)S(1)}, bf16[1,2,1408]{2,1,0:T(2,128)(2,1)S(1)}, u32[]{:S(2)}, u32[]{:S(2)}) collective-permute-start(bf16[1,2,1408]{2,1,0:T(2,128)(2,1)S(1)} %get-tuple-element.8), channel_id=1, source_target_pairs={{0,1},{1,2},{2,3},{3,4},{4,5},{5,6},{6,7},{7,8},{8,9},{9,10},{10,1... | collective-permute-start | bytes 16904 | tf_op jit(solution)/shard_map/ppermute | solution.py:19
  22.3 0.7 collective-permute-done
  23.1 1.4 fusion.48
  24.5 6.0 fusion.20
  30.5 426.3 %all-gather.5.cloned.1.call-done = bf16[5,1408,1536]{2,0,1:T(8,128)(2,1)} async-done(((bf16[5,44,1536]{2,0,1:T(8,128)(2,1)}), bf16[5,1408,1536]{2,0,1:T(8,128)(2,1)}) %all-gather.5.cloned.1.call-update) | async-done | bytes 21626896 | tf_op jit(solution)/shard_map/all_gather | solution.py:73
  456.8 92.6 %fusion.83 = (bf16[1,1408,1536]{2,0,1:T(2,128)(2,1)S(1)}, bf16[1,1408,1536]{2,0,1:T(2,128)(2,1)S(1)}, bf16[1,1408,1536]{2,0,1:T(2,128)(2,1)}, bf16[1,1408,1536]{2,0,1:T(2,128)(2,1)}, bf16[1,1408,1536]{2,0,1:T(2,128)(2,1)}) fusion(bf16[5,1408,1536]{2,0,1:T(8,128)(2,1)} %all-gather.5.cloned.1.call-done), kind=kLoop, calls=%fused_computation.101 | loop fusion | bytes 43253760 | tf_op jit(solution)/shard_map/slice | solution.py:37
  549.4 5.0 fusion.7
  554.5 4.9 fusion.9
  559.4 1.4 fusion.10
  560.8 0.0 copy-start.1
  560.8 1.4 fusion.11
  562.3 2.3 fusion.13
  564.6 2.9 reshape.58
  567.5 3.0 reduce_max.9
  570.5 0.2 multiply_reduce_fusion
  570.7 2.3 convolution_convert_fusion
  573.0 0.0 all-gather.7.cloned.1.call-update
  573.0 0.1 bitcast_reduce_fusion
  573.2 1.4 convolution_convert_fusion.1
  574.6 105.2 %all-gather.1 = bf16[256,128]{1,0:T(8,128)(2,1)S(1)} all-gather(bf16[8,128]{1,0:T(8,128)(2,1)S(1)} %get-tuple-element.11), channel_id=3, replica_groups=mesh['dp'=8,'seq'=16,'mp'=2] {'seq','mp'}, dimensions={0}, use_global_device_ids=true | all-gather | bytes 67584 | tf_op jit(solution)/shard_map/all_gather | solution.py:98
  679.8 0.1 fusion.55
  680.0 0.5 copy-done.3
  680.5 1.1 copy.31
  681.6 4.6 all-to-all-start
  686.2 0.0 all-reduce.3.cloned.1.call-start
  686.3 0.7 broadcast_multiply_fusion
  686.9 0.1 broadcast_bitcast_fusion
  687.0 1.3 fusion.52
  688.3 1.8 reshape.59
  690.1 9.7 %all-to-all-done = bf16[1,8,256,128]{3,1,0,2:T(8,128)(2,1)} async-done(((bf16[1,8,256,128]{3,1,0,2:T(8,128)(2,1)}), bf16[1,8,256,128]{3,1,0,2:T(8,128)(2,1)}, u32[]{:S(2)}, u32[]{:S(2)}) %all-to-all-start) | async-done | bytes 524320 | tf_op jit(solution)/shard_map/all_to_all | solution.py:104
  699.8 2.2 convolution_bitcast_fusion.1
  702.0 2.3 fusion.51
  704.4 0.0 all-reduce.3.cloned.1.call-update
  704.4 0.0 all-gather.7.cloned.1.call-done
  704.4 6.7 fusion
  711.1 5.9 fusion.63
  717.0 2.0 copy.30
  719.0 2.3 reshape.60
  721.3 4.0 fusion.15
  725.3 225.9 %all-reduce.3.cloned.1.call-done = f32[128,128]{1,0:T(8,128)} async-done(((f32[128,128]{1,0:T(8,128)}), f32[128,128]{1,0:T(8,128)}) %all-reduce.3.cloned.1.call-update) | async-done | bytes 65552 | tf_op jit(solution)/shard_map/psum | solution.py:112
  951.2 1.5 copy.69
  (23 shorter events, 0.1 us)
Async XLA Ops:
  7.2 679.8 %copy-start = (bf16[1536,1024]{1,0:T(8,128)(2,1)S(1)}, bf16[1536,1024]{1,0:T(8,128)(2,1)}, u32[]{:S(2)}) copy-start(bf16[1536,1024]{1,0:T(8,128)(2,1)} %param.14) | copy-start | bytes 9437188
  7.2 449.6 %all-gather.5.cloned.1.call-start = ((), (), s32[]{:S(2)}) async-start(), calls=%async_computation.1 | async-start | bytes 35684352 | tf_op jit(solution)/shard_map/all_gather | solution.py:73
  9.9 694.5 %all-gather.7.cloned.1.call-start = ((), (), s32[]{:S(2)}) async-start(), calls=%async_computation.3 | async-start | bytes 2703360 | tf_op jit(solution)/shard_map/all_gather | solution.py:97
  10.7 11.6 %collective-permute-start.1 = (bf16[1,2,1408]{2,1,0:T(2,128)(2,1)S(1)}, bf16[1,2,1408]{2,1,0:T(2,128)(2,1)S(1)}, u32[]{:S(2)}, u32[]{:S(2)}) collective-permute-start(bf16[1,2,1408]{2,1,0:T(2,128)(2,1)S(1)} %get-tuple-element.9), channel_id=1, source_target_pairs={{1,0},{2,1},{3,2},{4,3},{5,4},{6,5},{7,6},{8,7},{9,8},{10,9},{11,1... | collective-permute-start | bytes 16904 | tf_op jit(solution)/shard_map/ppermute | solution.py:20
  12.0 11.0 %collective-permute-start = (bf16[1,2,1408]{2,1,0:T(2,128)(2,1)S(1)}, bf16[1,2,1408]{2,1,0:T(2,128)(2,1)S(1)}, u32[]{:S(2)}, u32[]{:S(2)}) collective-permute-start(bf16[1,2,1408]{2,1,0:T(2,128)(2,1)S(1)} %get-tuple-element.8), channel_id=1, source_target_pairs={{0,1},{1,2},{2,3},{3,4},{4,5},{5,6},{6,7},{7,8},{8,9},{9,10},{10,1... | collective-permute-start | bytes 16904 | tf_op jit(solution)/shard_map/ppermute | solution.py:19
  456.8 92.6 %copy-start.4 = (bf16[260,1408]{1,0:T(8,128)(2,1)S(1)}, bf16[260,1408]{1,0:T(8,128)(2,1)}, u32[]{:S(2)}) copy-start(bf16[260,1408]{1,0:T(8,128)(2,1)} %fusion.20) | copy-start | bytes 2196484
  549.4 9.9 %slice-start = ((s8[8650752]{0:T(1024)(128)(4,1)}), s8[4194304]{0:T(1024)(128)(4,1)S(1)}, s32[]{:S(2)}) async-start(s8[8650752]{0:T(1024)(128)(4,1)} %bitcast.79), calls=%async_computation.4 | async-start | bytes 8388608
  549.4 9.9 %slice-start.1 = ((s8[8650752]{0:T(1024)(128)(4,1)}), s8[4194304]{0:T(1024)(128)(4,1)S(1)}, s32[]{:S(2)}) async-start(s8[8650752]{0:T(1024)(128)(4,1)} %bitcast.79), calls=%async_computation.5 | async-start | bytes 8388608
  554.4 4.9 slice-start.2
  560.8 1.4 copy-start.1
  564.6 6.1 copy-start.5
  573.0 106.8 %copy-start.2 = (bf16[1,8,256,128]{3,2,1,0:T(8,128)(2,1)S(1)}, bf16[1,8,256,128]{3,2,1,0:T(8,128)(2,1)}, u32[]{:S(2)}) copy-start(bf16[1,8,256,128]{3,2,1,0:T(8,128)(2,1)} %param.19) | copy-start | bytes 1572868
  679.8 0.6 copy-start.3
  681.6 18.2 %all-to-all-start = ((bf16[1,8,256,128]{3,1,0,2:T(8,128)(2,1)}), bf16[1,8,256,128]{3,1,0,2:T(8,128)(2,1)}, u32[]{:S(2)}, u32[]{:S(2)}) async-start(bf16[1,8,256,128]{3,1,0,2:T(8,128)(2,1)} %copy.31), calls=%async_computation | async-start | bytes 1048576 | tf_op jit(solution)/shard_map/all_to_all | solution.py:104
  686.2 264.9 %all-reduce.3.cloned.1.call-start = ((), (), s32[]{:S(2)}) async-start(), calls=%async_computation.2 | async-start | bytes 131072 | tf_op jit(solution)/shard_map/psum | solution.py:112
  704.4 6.7 copy-start.6
Sparse Core Ops, SparseCore 0:
  11.4 445.3 all-gather.4
  573.2 103.0 all-gather.6
  704.5 246.6 all-reduce.2
where the time goes:
time: 960 us; the launch traced here: 959 us
  waiting for transfers between devices  663 us (69%)
  local copies, waits for them, and re-layouts  108 us (11%)
  blocking collectives  105 us (11%)
  matrix products  41.2 us (4%)
  starting transfers between devices  16.3 us (2%)
  between operations  14 us (1%)
  other arithmetic  11.6 us (1%)
    all_gather x1, waiting for transfers between devices, per_device(): lax.all_gather(conv_weight, ('seq', 'mp'), axis=1, tiled=True)  426 us
    psum x1, waiting for transfers between devices, per_device(): grad_flip = lax.psum(grad_term, ('dp', 'seq', 'mp'))  226 us
    all_gather x1, blocking collectives, per_device(): lax.all_gather(pair_k[None], ('seq', 'mp'), axis=1, tiled=True)  105 us
    slice x1, local copies, waits for them, and re-layouts, tap_sum(): filter_rows[lag_index]  92.6 us
  transfers between devices with their start and end apart: 6, of which 4 were waited for; matrix products, arithmetic and copies ran while one was open for 4% of the time, Pallas kernels for 0%

commit v1 on v0

--- a/solution.py
+++ b/solution.py
@@ -109,7 +109,9 @@
     grad_term = jnp.einsum(
         "bac,abd->cd", flipped, pair_cotangent[0], preferred_element_type=jnp.float32
     )
-    grad_flip = lax.psum(grad_term, ("dp", "seq", "mp"))
+    grad_flip = grad_term
+    for d in ("dp", ("seq", "mp")):
+        grad_flip = jax.lax.psum(grad_flip, d)
     key_rows = keys_all[0][:, :key_dim]
     value_rows = keys_all[0][:, key_dim:]
     query_rows = queries.reshape(coarse_rows * head_count, key_dim)

time: 960 us -> 1280 us (1.33); the launches traced: 959 us -> 1260 us
  waiting for transfers between devices: 663 us -> 972 us
    psum x1 -> x2, waiting for transfers between devices: 226 us -> 420 us  [per_device(): grad_flip = jax.lax.psum(grad_flip, d)]
    all_gather x1, waiting for transfers between devices: 0.02 us -> 111 us  [per_device(): lax.all_gather(keyvals[None], ('seq', 'mp'), axis=1, tiled=True)]
  transfers between devices with their start and end apart: 6 -> 7, of which waited for: 4 -> 6; matrix products, arithmetic and copies ran while one was open for 4% -> 3% of each run, Pallas kernels for 0% -> 0%
where the time goes in v1:
time: 1280 us; the launch traced here: 1260 us
  waiting for transfers between devices  972 us (76%)
  local copies, waits for them, and re-layouts  108 us (8%)
  blocking collectives  96.4 us (8%)
  matrix products  41.2 us (3%)
  starting transfers between devices  16.5 us (1%)
  between operations  14 us (1%)
    all_gather x1, waiting for transfers between devices, per_device(): lax.all_gather(conv_weight, ('seq', 'mp'), axis=1, tiled=True)  426 us
    psum x2, waiting for transfers between devices, per_device(): grad_flip = jax.lax.psum(grad_flip, d)  420 us
    all_gather x1, waiting for transfers between devices, per_device(): lax.all_gather(keyvals[None], ('seq', 'mp'), axis=1, tiled=True)  111 us
    all_gather x1, blocking collectives, per_device(): lax.all_gather(pair_k[None], ('seq', 'mp'), axis=1, tiled=True)  96.4 us
    slice x1, local copies, waits for them, and re-layouts, tap_sum(): filter_rows[lag_index]  92.6 us
  transfers between devices with their start and end apart: 7, of which 6 were waited for; matrix products, arithmetic and copies ran while one was open for 3% of the time, Pallas kernels for 0%

profile of v1, /device:TPU:1, one launch (start us, length us, event | category | flops | bytes accessed | tf_op | source)
XLA Modules:
  0.0 1259.9 jit_solution(4507708547094996088)
XLA Ops:
  7.2 0.0 all-gather.5.cloned.1.call-start
  7.2 2.7 copy.24
  9.9 0.0 all-gather.5.cloned.1.call-update
  9.9 0.8 fusion.84
  10.7 1.3 collective-permute-start.1
  12.0 10.3 collective-permute-start
  22.3 0.7 collective-permute-done
  23.0 1.4 fusion.48
  24.5 6.0 fusion.20
  30.4 426.4 %all-gather.5.cloned.1.call-done = bf16[5,1408,1536]{2,0,1:T(8,128)(2,1)} async-done(((bf16[5,44,1536]{2,0,1:T(8,128)(2,1)}), bf16[5,1408,1536]{2,0,1:T(8,128)(2,1)}) %all-gather.5.cloned.1.call-update) | async-done | bytes 21626896 | tf_op jit(solution)/shard_map/all_gather | solution.py:73
  456.8 92.6 %fusion.83 = (bf16[1,1408,1536]{2,0,1:T(2,128)(2,1)S(1)}, bf16[1,1408,1536]{2,0,1:T(2,128)(2,1)S(1)}, bf16[1,1408,1536]{2,0,1:T(2,128)(2,1)}, bf16[1,1408,1536]{2,0,1:T(2,128)(2,1)}, bf16[1,1408,1536]{2,0,1:T(2,128)(2,1)}) fusion(bf16[5,1408,1536]{2,0,1:T(8,128)(2,1)} %all-gather.5.cloned.1.call-done), kind=kLoop, calls=%fused_computation.101 | loop fusion | bytes 43253760 | tf_op jit(solution)/shard_map/slice | solution.py:37
  549.4 5.0 fusion.7
  554.5 4.9 fusion.9
  559.4 1.4 fusion.10
  560.8 1.4 fusion.11
  562.3 2.3 fusion.13
  564.6 2.8 reshape.58
  567.5 3.0 reduce_max.9
  570.5 0.1 bitcast_reduce_fusion
  570.6 1.4 convolution_convert_fusion.1
  572.0 96.4 %all-gather.1 = bf16[256,128]{1,0:T(8,128)(2,1)S(1)} all-gather(bf16[8,128]{1,0:T(8,128)(2,1)S(1)} %get-tuple-element.11), channel_id=3, replica_groups=mesh['dp'=8,'seq'=16,'mp'=2] {'seq','mp'}, dimensions={0}, use_global_device_ids=true | all-gather | bytes 67584 | tf_op jit(solution)/shard_map/all_gather | solution.py:98
  668.5 0.1 fusion.55
  668.6 0.5 copy-done.3
  669.1 1.1 copy.31
  670.2 4.8 all-to-all-start
  675.0 0.0 all-reduce.4.cloned.1.call-start
  675.0 0.2 multiply_reduce_fusion
  675.2 13.4 %all-to-all-done = bf16[1,8,256,128]{3,1,0,2:T(8,128)(2,1)} async-done(((bf16[1,8,256,128]{3,1,0,2:T(8,128)(2,1)}), bf16[1,8,256,128]{3,1,0,2:T(8,128)(2,1)}, u32[]{:S(2)}, u32[]{:S(2)}) %all-to-all-start) | async-done | bytes 524320 | tf_op jit(solution)/shard_map/all_to_all | solution.py:104
  688.6 2.2 convolution_bitcast_fusion.1
  690.8 0.0 all-reduce.4.cloned.1.call-update
  690.8 0.0 all-gather.7.cloned.1.call-start
  690.9 2.3 convolution_convert_fusion
  693.2 0.0 all-gather.7.cloned.1.call-update
  693.2 0.0 all-reduce.6.cloned.1.call-start
  693.3 0.7 broadcast_multiply_fusion
  693.9 0.1 broadcast_bitcast_fusion
  694.0 1.3 fusion.52
  695.3 1.8 reshape.59
  697.1 2.3 fusion.51
  699.4 66.9 %all-reduce.4.cloned.1.call-done = f32[128,128]{1,0:T(8,128)} async-done(((f32[128,128]{1,0:T(8,128)}), f32[128,128]{1,0:T(8,128)}) %all-reduce.4.cloned.1.call-update) | async-done | bytes 65552 | tf_op jit(solution)/shard_map/psum | solution.py:114
  766.3 111.3 %all-gather.7.cloned.1.call-done = bf16[4096,320]{0,1:T(8,128)(2,1)} async-done(((bf16[128,320]{0,1:T(8,128)(2,1)}), bf16[4096,320]{0,1:T(8,128)(2,1)}) %all-gather.7.cloned.1.call-update) | async-done | bytes 2621456 | tf_op jit(solution)/shard_map/all_gather | solution.py:97
  877.7 6.6 fusion
  884.3 5.9 fusion.63
  890.3 2.0 copy.30
  892.3 2.3 reshape.60
  894.5 4.0 fusion.15
  898.6 353.4 %all-reduce.6.cloned.1.call-done = f32[128,128]{1,0:T(8,128)} async-done(((f32[128,128]{1,0:T(8,128)}), f32[128,128]{1,0:T(8,128)}) %all-reduce.6.cloned.1.call-update) | async-done | bytes 65552 | tf_op jit(solution)/shard_map/psum | solution.py:114
  1251.9 1.5 copy.70
  (26 shorter events, 0.1 us)
Async XLA Ops:
  7.2 686.8 %copy-start = (bf16[1536,1024]{1,0:T(8,128)(2,1)S(1)}, bf16[1536,1024]{1,0:T(8,128)(2,1)}, u32[]{:S(2)}) copy-start(bf16[1536,1024]{1,0:T(8,128)(2,1)} %param.14) | copy-start | bytes 9437188
  7.2 449.6 %all-gather.5.cloned.1.call-start = ((), (), s32[]{:S(2)}) async-start(), calls=%async_computation.1 | async-start | bytes 35684352 | tf_op jit(solution)/shard_map/all_gather | solution.py:73
  10.7 11.6 collective-permute-start.1
  12.0 11.0 collective-permute-start
  456.8 92.6 %copy-start.4 = (bf16[260,1408]{1,0:T(8,128)(2,1)S(1)}, bf16[260,1408]{1,0:T(8,128)(2,1)}, u32[]{:S(2)}) copy-start(bf16[260,1408]{1,0:T(8,128)(2,1)} %fusion.20) | copy-start | bytes 2196484
  549.4 9.9 slice-start
  549.4 9.9 slice-start.1
  554.4 4.9 slice-start.2
  560.8 1.4 copy-start.1
  570.5 98.0 %copy-start.2 = (bf16[1,8,256,128]{3,2,1,0:T(8,128)(2,1)S(1)}, bf16[1,8,256,128]{3,2,1,0:T(8,128)(2,1)}, u32[]{:S(2)}) copy-start(bf16[1,8,256,128]{3,2,1,0:T(8,128)(2,1)} %param.19) | copy-start | bytes 1572868
  668.4 0.6 copy-start.3
  670.2 20.6 %copy-start.5 = (f32[1536]{0:T(1024)S(1)}, f32[1536]{0:T(1024)}, u32[]{:S(2)}) copy-start(f32[1536]{0:T(1024)} %param.13) | copy-start | bytes 18436
  670.2 18.4 %all-to-all-start = ((bf16[1,8,256,128]{3,1,0,2:T(8,128)(2,1)}), bf16[1,8,256,128]{3,1,0,2:T(8,128)(2,1)}, u32[]{:S(2)}, u32[]{:S(2)}) async-start(bf16[1,8,256,128]{3,1,0,2:T(8,128)(2,1)} %copy.31), calls=%async_computation | async-start | bytes 1048576 | tf_op jit(solution)/shard_map/all_to_all | solution.py:104
  675.0 91.3 %all-reduce.4.cloned.1.call-start = ((), (), s32[]{:S(2)}) async-start(), calls=%async_computation.2 | async-start | bytes 131072 | tf_op jit(solution)/shard_map/psum | solution.py:114
  690.8 186.9 %all-gather.7.cloned.1.call-start = ((), (), s32[]{:S(2)}) async-start(), calls=%async_computation.4 | async-start | bytes 2703360 | tf_op jit(solution)/shard_map/all_gather | solution.py:97
  693.2 558.7 %all-reduce.6.cloned.1.call-start = ((), (), s32[]{:S(2)}) async-start(), calls=%async_computation.3 | async-start | bytes 131072 | tf_op jit(solution)/shard_map/psum | solution.py:114
  877.7 6.7 copy-start.6
Sparse Core Ops, SparseCore 0:
  11.4 445.3 all-gather.4
  690.9 75.3 all-reduce.3
  770.0 107.6 all-gather.6
  880.3 371.5 all-reduce.5
